TPU v7x, 256 devices: a whole 4x4x8 slice. The times are simulated.
256 devices in a mesh: ta: 8 (over z), ha: 4 (over x_hi, core), wa: 8 (over x_lo, y).
Axes of the slice: x: 4 (x_hi: 2, x_lo: 2; x = x_hi * 2 + x_lo), y: 4, z: 8, core: 2. Of those that a mesh axis runs over, the one named last changes fastest.
Arguments:
- features: bfloat16 [32, 64, 128, 256], P('ta', 'ha', 'wa'), may hold values from -6 to 6
- norm_gain: float32 [256], replicated, may hold values from 0.5 to 1.5
- conv_weight: bfloat16 [3, 3, 3, 256, 256], replicated, may hold values from -0.078125 to 0.078125
- cotangent: bfloat16 [32, 64, 128, 256], P('ta', 'ha', 'wa'), may hold values from -6 to 6
Outputs:
- decoded: bfloat16 [32, 64, 128, 256], P('ta', 'ha', 'wa')
- grad_features: bfloat16 [32, 64, 128, 256], P('ta', 'ha', 'wa')
- grad_weight: float32 [3, 3, 3, 256, 256], P(None, None, None, None, ('ha', 'wa'))
All inputs are finite; a program needn't handle non-finite values.
Results may differ from a plain program's by a relative error of at most 0.0032.
Values may be sent and summed in bfloat16 or wider, within the bound.
A program may use at most 128 MiB of HBM per device.

v0:
```python
import jax
import jax.numpy as jnp
from jax import lax
from jax.sharding import PartitionSpec as P

EPSILON = 1e-06


def from_behind(array, axis, by):
    length = lax.axis_size(axis)
    pairs = [(i, i + by) for i in range(length) if 0 <= i + by < length]
    return lax.ppermute(array, axis, pairs)


def with_halo(cells, sides, width):
    for axis, dim in sides:
        count = lax.axis_size(axis)
        ends = count - 1
        head = lax.slice_in_dim(cells, 0, width, axis=dim)
        tail = lax.slice_in_dim(cells, cells.shape[dim] - width, cells.shape[dim], axis=dim)
        cells = jnp.concatenate(
            [
                lax.ppermute(tail, axis, [(i, (i + 1) % count) for i in range(ends)]),
                cells,
                lax.ppermute(head, axis, [((i + 1) % count, i) for i in range(ends)]),
            ],
            axis=dim,
        )
    return cells


def activate(features, norm_gain):
    values = features.astype(jnp.float32)
    inverse = lax.rsqrt(jnp.mean(values * values, axis=-1, keepdims=True) + EPSILON)
    unit_rms = values * inverse
    normed = unit_rms * norm_gain
    activated = (normed * jax.nn.sigmoid(normed)).astype(jnp.bfloat16)
    return (values, inverse, unit_rms, normed, activated)


def norm_backward(grad_act, normed, unit_rms, inverse, norm_gain):
    logistic = jax.nn.sigmoid(normed)
    grad_normed = grad_act * logistic * (1.0 + normed * (1.0 - logistic))
    grad_unit = grad_normed * norm_gain
    return inverse * (grad_unit - unit_rms * jnp.mean(grad_unit * unit_rms, axis=-1, keepdims=True))


def body(features, norm_gain, conv_weight, cotangent):
    frames, height, width, channels = features.shape
    values, inverse, unit_rms, normed, activated = activate(features, norm_gain)
    earlier = from_behind(activated[frames - 2 :], "ta", 1)
    padded = with_halo(jnp.concatenate([earlier, activated], 0), (("ha", 1), ("wa", 2)), 1)
    later = from_behind(cotangent[:2], "ta", -1)
    grad_padded = with_halo(jnp.concatenate([cotangent, later], 0), (("ha", 1), ("wa", 2)), 1)
    flat_grad = cotangent.reshape(-1, channels)
    mixed = jnp.zeros((frames * height * width, channels), jnp.float32)
    grad_act = jnp.zeros((frames * height * width, channels), jnp.float32)
    windows = []
    for t_off in range(3):
        for h_off in range(3):
            for w_off in range(3):
                window = padded[
                    t_off : t_off + frames, h_off : h_off + height, w_off : w_off + width
                ].reshape(-1, channels)
                windows.append(window)
                mixed = mixed + jnp.dot(
                    window, conv_weight[t_off, h_off, w_off], preferred_element_type=jnp.float32
                )
                back = grad_padded[
                    2 - t_off : 2 - t_off + frames,
                    2 - h_off : 2 - h_off + height,
                    2 - w_off : 2 - w_off + width,
                ].reshape(-1, channels)
                grad_act = grad_act + lax.dot_general(
                    back,
                    conv_weight[t_off, h_off, w_off],
                    (((1,), (1,)), ((), ())),
                    preferred_element_type=jnp.float32,
                )
    owners = lax.axis_size("ha") * lax.axis_size("wa")
    owned = channels // owners
    weight_taps = jnp.stack(
        [
            lax.dot_general(
                window, flat_grad, (((0,), (0,)), ((), ())), preferred_element_type=jnp.float32
            )
            for window in windows
        ]
    )
    shared = lax.psum_scatter(weight_taps, ("ha", "wa"), scatter_dimension=2, tiled=True)
    summed = lax.psum(shared, "ta")
    voxels_all = (
        frames * height * width * lax.axis_size("ta") * lax.axis_size("ha") * lax.axis_size("wa")
    )
    grad_weight = summed.reshape(3, 3, 3, channels, owned) * float(voxels_all) ** (-0.5)
    decoded = (values + mixed.reshape(features.shape)).astype(jnp.bfloat16)
    grad_norm = norm_backward(
        grad_act.reshape(features.shape), normed, unit_rms, inverse, norm_gain
    )
    grad_features = (cotangent.astype(jnp.float32) + grad_norm).astype(jnp.bfloat16)
    return (decoded, grad_features, grad_weight)


def solution(mesh):
    placed = (P("ta", "ha", "wa", None), P(), P(), P("ta", "ha", "wa", None))
    return jax.shard_map(
        body,
        mesh=mesh,
        in_specs=placed,
        out_specs=(
            P("ta", "ha", "wa", None),
            P("ta", "ha", "wa", None),
            P(None, None, None, None, ("ha", "wa")),
        ),
        check_vma=False,
    )
```

profile of v0, /device:TPU:1, one launch (start us, length us, event | category | flops | bytes accessed | tf_op | source)
XLA Modules:
  0.0 360.2 jit_solution(647792730584632596)
XLA Ops:
  8.2 1.3 collective-permute-start.5
  9.5 1.1 constant_dynamic-update-slice_fusion.1
  10.6 1.3 fusion.49
  11.8 4.9 %collective-permute-done.5 = bf16[2,16,16,256]{3,2,1,0:T(8,128)(2,1)S(1)} collective-permute-done((bf16[2,16,16,256]{3,2,1,0:T(8,128)(2,1)S(1)}, bf16[2,16,16,256]{3,2,1,0:T(8,128)(2,1)S(1)}, u32[]{:S(2)}, u32[]{:S(2)}) %collective-permute-start.5) | collective-permute-done | bytes 262176 | tf_op jit(solution)/shard_map/ppermute | solution.py:12
  16.8 7.6 %collective-permute-start.6 = (bf16[6,1,16,256]{3,2,1,0:T(8,128)(2,1)S(1)}, bf16[6,1,16,256]{3,2,1,0:T(8,128)(2,1)S(1)}, u32[]{:S(2)}, u32[]{:S(2)}) collective-permute-start(bf16[6,1,16,256]{3,2,1,0:T(8,128)(2,1)S(1)} %get-tuple-element.70), channel_id=1, source_target_pairs={{0,8},{8,16},{16,24},{1,9},{9,17},{17,25},{2,10},{10,18},{18,26},{... | collective-permute-start | bytes 147464 | tf_op jit(solution)/shard_map/ppermute | solution.py:23
  24.4 1.9 collective-permute-start.7
  26.4 4.9 %collective-permute-done.7 = bf16[6,1,16,256]{3,2,1,0:T(8,128)(2,1)S(1)} collective-permute-done((bf16[6,1,16,256]{3,2,1,0:T(8,128)(2,1)S(1)}, bf16[6,1,16,256]{3,2,1,0:T(8,128)(2,1)S(1)}, u32[]{:S(2)}, u32[]{:S(2)}) %collective-permute-start.7) | collective-permute-done | bytes 49184 | tf_op jit(solution)/shard_map/ppermute | solution.py:25
  31.5 1.3 collective-permute-start.8
  32.8 4.0 %collective-permute-start.9 = (bf16[6,18,1,256]{3,2,1,0:T(2,128)(2,1)S(1)}, bf16[6,18,1,256]{3,2,1,0:T(2,128)(2,1)S(1)}, u32[]{:S(2)}, u32[]{:S(2)}) collective-permute-start(bf16[6,18,1,256]{3,2,1,0:T(2,128)(2,1)S(1)} %get-tuple-element.48), channel_id=1, source_target_pairs={{0,1},{1,2},{2,3},{3,4},{4,5},{5,6},{6,7},{8,9},{9,10},{10,11},{11... | collective-permute-start | bytes 165896 | tf_op jit(solution)/shard_map/ppermute | solution.py:23
  39.4 3.3 fusion.191
  52.9 1.6 fusion.48
  54.5 3.6 collective-permute-start
  58.0 4.0 %collective-permute-done = bf16[2,16,16,256]{3,2,1,0:T(8,128)(2,1)S(1)} collective-permute-done((bf16[2,16,16,256]{3,2,1,0:T(8,128)(2,1)S(1)}, bf16[2,16,16,256]{3,2,1,0:T(8,128)(2,1)S(1)}, u32[]{:S(2)}, u32[]{:S(2)}) %collective-permute-start) | collective-permute-done | bytes 262176 | tf_op jit(solution)/shard_map/ppermute | solution.py:12
  62.0 1.9 collective-permute-start.2
  63.9 5.1 %collective-permute-start.1 = (bf16[6,1,16,256]{3,2,1,0:T(8,128)(2,1)S(1)}, bf16[6,1,16,256]{3,2,1,0:T(8,128)(2,1)S(1)}, u32[]{:S(2)}, u32[]{:S(2)}) collective-permute-start(bf16[6,1,16,256]{3,2,1,0:T(8,128)(2,1)S(1)} %get-tuple-element.77), channel_id=1, source_target_pairs={{0,8},{8,16},{16,24},{1,9},{9,17},{17,25},{2,10},{10,18},{18,26},{... | collective-permute-start | bytes 147464 | tf_op jit(solution)/shard_map/ppermute | solution.py:23
  69.1 1.1 collective-permute-done.1
  70.4 1.3 collective-permute-start.4
  71.7 4.9 %collective-permute-start.3 = (bf16[6,18,1,256]{3,2,1,0:T(2,128)(2,1)S(1)}, bf16[6,18,1,256]{3,2,1,0:T(2,128)(2,1)S(1)}, u32[]{:S(2)}, u32[]{:S(2)}) collective-permute-start(bf16[6,18,1,256]{3,2,1,0:T(2,128)(2,1)S(1)} %get-tuple-element.52), channel_id=1, source_target_pairs={{0,1},{1,2},{2,3},{3,4},{4,5},{5,6},{6,7},{8,9},{9,10},{10,11},{11... | collective-permute-start | bytes 165896 | tf_op jit(solution)/shard_map/ppermute | solution.py:23
  76.6 1.5 collective-permute-done.3
  79.1 1.1 fusion.30
  80.1 1.1 fusion.36
  86.4 1.1 fusion.35
  93.7 1.1 fusion.21
  95.8 1.1 fusion.33
  96.9 1.1 fusion.19
  105.3 1.1 fusion.31
  107.4 10.3 %copy.10 = f32[27,256,256]{1,0,2:T(8,128)} copy(f32[27,256,256]{2,1,0:T(8,128)} %fusion.12) | data formatting | bytes 14155776 | tf_op jit(solution)/shard_map/stack | solution.py:82
  118.4 1.6 copy-done.1
  129.6 148.3 %reduce-scatter.2.cloned.1.call-done = f32[27,256,8]{1,0,2:T(8,128)} async-done(((f32[27,256,256]{1,0,2:T(8,128)}), f32[27,256,8]{1,0,2:T(8,128)}) %reduce-scatter.2.cloned.1.call-update) | async-done | bytes 221200 | tf_op jit(solution)/shard_map/reduce_scatter | solution.py:90
  277.9 1.8 copy.11
  280.7 71.0 %all-reduce.2.cloned.1.call-done = f32[27,256,8]{1,2,0:T(8,128)} async-done(((f32[27,256,8]{1,2,0:T(8,128)}), f32[27,256,8]{1,2,0:T(8,128)}) %all-reduce.2.cloned.1.call-update) | async-done | bytes 221200 | tf_op jit(solution)/shard_map/psum | solution.py:91
  351.7 1.6 broadcast_multiply_fusion
  (114 shorter events, 46.8 us)
Async XLA Ops:
  7.2 270.8 %reduce-scatter.2.cloned.1.call-start = ((), (), s32[]{:S(2)}) async-start(), calls=%async_computation.1 | async-start | bytes 8650752 | tf_op jit(solution)/shard_map/reduce_scatter | solution.py:90
  8.2 8.6 %collective-permute-start.5 = (bf16[2,16,16,256]{3,2,1,0:T(8,128)(2,1)S(1)}, bf16[2,16,16,256]{3,2,1,0:T(8,128)(2,1)S(1)}, u32[]{:S(2)}, u32[]{:S(2)}) collective-permute-start(bf16[2,16,16,256]{3,2,1,0:T(8,128)(2,1)S(1)} %slice.400), channel_id=1, source_target_pairs={{32,0},{64,32},{96,64},{128,96},{160,128},{192,160},{224,192},{33,... | collective-permute-start | bytes 786440 | tf_op jit(solution)/shard_map/ppermute | solution.py:12
  16.8 9.6 %collective-permute-start.6 = (bf16[6,1,16,256]{3,2,1,0:T(8,128)(2,1)S(1)}, bf16[6,1,16,256]{3,2,1,0:T(8,128)(2,1)S(1)}, u32[]{:S(2)}, u32[]{:S(2)}) collective-permute-start(bf16[6,1,16,256]{3,2,1,0:T(8,128)(2,1)S(1)} %get-tuple-element.70), channel_id=1, source_target_pairs={{0,8},{8,16},{16,24},{1,9},{9,17},{17,25},{2,10},{10,18},{18,26},{... | collective-permute-start | bytes 147464 | tf_op jit(solution)/shard_map/ppermute | solution.py:23
  24.4 6.9 %collective-permute-start.7 = (bf16[6,1,16,256]{3,2,1,0:T(8,128)(2,1)S(1)}, bf16[6,1,16,256]{3,2,1,0:T(8,128)(2,1)S(1)}, u32[]{:S(2)}, u32[]{:S(2)}) collective-permute-start(bf16[6,1,16,256]{3,2,1,0:T(8,128)(2,1)S(1)} %get-tuple-element.71), channel_id=1, source_target_pairs={{8,0},{16,8},{24,16},{9,1},{17,9},{25,17},{10,2},{18,10},{26,18},{... | collective-permute-start | bytes 147464 | tf_op jit(solution)/shard_map/ppermute | solution.py:25
  26.3 11.0 %copy-start = (bf16[3,3,3,256,256]{4,3,2,1,0:T(8,128)(2,1)S(1)}, bf16[3,3,3,256,256]{4,3,2,1,0:T(8,128)(2,1)}, u32[]{:S(2)}) copy-start(bf16[3,3,3,256,256]{4,3,2,1,0:T(8,128)(2,1)} %param.6) | copy-start | bytes 10616836
  31.5 6.2 %collective-permute-start.8 = (bf16[6,18,1,256]{3,2,1,0:T(2,128)(2,1)S(1)}, bf16[6,18,1,256]{3,2,1,0:T(2,128)(2,1)S(1)}, u32[]{:S(2)}, u32[]{:S(2)}) collective-permute-start(bf16[6,18,1,256]{3,2,1,0:T(2,128)(2,1)S(1)} %get-tuple-element.47), channel_id=1, source_target_pairs={{1,0},{2,1},{3,2},{4,3},{5,4},{6,5},{7,6},{9,8},{10,9},{11,10},{12... | collective-permute-start | bytes 165896 | tf_op jit(solution)/shard_map/ppermute | solution.py:25
  32.8 5.7 %collective-permute-start.9 = (bf16[6,18,1,256]{3,2,1,0:T(2,128)(2,1)S(1)}, bf16[6,18,1,256]{3,2,1,0:T(2,128)(2,1)S(1)}, u32[]{:S(2)}, u32[]{:S(2)}) collective-permute-start(bf16[6,18,1,256]{3,2,1,0:T(2,128)(2,1)S(1)} %get-tuple-element.48), channel_id=1, source_target_pairs={{0,1},{1,2},{2,3},{3,4},{4,5},{5,6},{6,7},{8,9},{9,10},{10,11},{11... | collective-permute-start | bytes 165896 | tf_op jit(solution)/shard_map/ppermute | solution.py:23
  49.4 1.0 copy-start.4
  51.1 1.0 copy-start.2
  51.1 1.0 copy-start.5
  54.5 7.5 %collective-permute-start = (bf16[2,16,16,256]{3,2,1,0:T(8,128)(2,1)S(1)}, bf16[2,16,16,256]{3,2,1,0:T(8,128)(2,1)S(1)}, u32[]{:S(2)}, u32[]{:S(2)}) collective-permute-start(bf16[2,16,16,256]{3,2,1,0:T(8,128)(2,1)S(1)} %slice.431), channel_id=1, source_target_pairs={{0,32},{32,64},{64,96},{96,128},{128,160},{160,192},{192,224},{1,3... | collective-permute-start | bytes 786440 | tf_op jit(solution)/shard_map/ppermute | solution.py:12
  62.0 7.1 %collective-permute-start.2 = (bf16[6,1,16,256]{3,2,1,0:T(8,128)(2,1)S(1)}, bf16[6,1,16,256]{3,2,1,0:T(8,128)(2,1)S(1)}, u32[]{:S(2)}, u32[]{:S(2)}) collective-permute-start(bf16[6,1,16,256]{3,2,1,0:T(8,128)(2,1)S(1)} %get-tuple-element.76), channel_id=1, source_target_pairs={{8,0},{16,8},{24,16},{9,1},{17,9},{25,17},{10,2},{18,10},{26,18},{... | collective-permute-start | bytes 147464 | tf_op jit(solution)/shard_map/ppermute | solution.py:25
  63.9 6.3 %collective-permute-start.1 = (bf16[6,1,16,256]{3,2,1,0:T(8,128)(2,1)S(1)}, bf16[6,1,16,256]{3,2,1,0:T(8,128)(2,1)S(1)}, u32[]{:S(2)}, u32[]{:S(2)}) collective-permute-start(bf16[6,1,16,256]{3,2,1,0:T(8,128)(2,1)S(1)} %get-tuple-element.77), channel_id=1, source_target_pairs={{0,8},{8,16},{16,24},{1,9},{9,17},{17,25},{2,10},{10,18},{18,26},{... | collective-permute-start | bytes 147464 | tf_op jit(solution)/shard_map/ppermute | solution.py:23
  70.4 6.2 %collective-permute-start.4 = (bf16[6,18,1,256]{3,2,1,0:T(2,128)(2,1)S(1)}, bf16[6,18,1,256]{3,2,1,0:T(2,128)(2,1)S(1)}, u32[]{:S(2)}, u32[]{:S(2)}) collective-permute-start(bf16[6,18,1,256]{3,2,1,0:T(2,128)(2,1)S(1)} %get-tuple-element.51), channel_id=1, source_target_pairs={{1,0},{2,1},{3,2},{4,3},{5,4},{6,5},{7,6},{9,8},{10,9},{11,10},{12... | collective-permute-start | bytes 165896 | tf_op jit(solution)/shard_map/ppermute | solution.py:25
  71.7 6.4 %collective-permute-start.3 = (bf16[6,18,1,256]{3,2,1,0:T(2,128)(2,1)S(1)}, bf16[6,18,1,256]{3,2,1,0:T(2,128)(2,1)S(1)}, u32[]{:S(2)}, u32[]{:S(2)}) collective-permute-start(bf16[6,18,1,256]{3,2,1,0:T(2,128)(2,1)S(1)} %get-tuple-element.52), channel_id=1, source_target_pairs={{0,1},{1,2},{2,3},{3,4},{4,5},{5,6},{6,7},{8,9},{9,10},{10,11},{11... | collective-permute-start | bytes 165896 | tf_op jit(solution)/shard_map/ppermute | solution.py:23
  117.7 234.0 %all-reduce.2.cloned.1.call-start = ((), (), s32[]{:S(2)}) async-start(), calls=%async_computation.2 | async-start | bytes 442368 | tf_op jit(solution)/shard_map/psum | solution.py:91
  118.0 2.0 copy-start.1
  129.0 150.7 %copy-start.3 = (bf16[4,16,16,256]{3,2,1,0:T(8,128)(2,1)S(1)}, bf16[4,16,16,256]{3,2,1,0:T(8,128)(2,1)}, u32[]{:S(2)}) copy-start(bf16[4,16,16,256]{3,2,1,0:T(8,128)(2,1)} %param.4) | copy-start | bytes 1572868
Sparse Core Ops, SparseCore 0:
  117.8 160.0 reduce-scatter.1
  280.8 70.8 all-reduce.1
where the time goes:
time: 365 us; the launch traced here: 360 us
  waiting for transfers between devices  237 us (65%)
  matrix products  45.1 us (12%)
  starting transfers between devices  33.2 us (9%)
  local copies, waits for them, and re-layouts  21.4 us (6%)
  between operations  14.7 us (4%)
  other arithmetic  9.12 us (2%)
    reduce_scatter x1, waiting for transfers between devices, body(): lax.psum_scatter(weight_taps, ('ha', 'wa'), scatter_dimension=2, tiled=True)  148 us
    psum x1, waiting for transfers between devices, body(): summed = lax.psum(shared, 'ta')  71 us
    dot_general x27, matrix products, body(): lax.dot_general(window, flat_grad, (((0,), (0,)), ((), ())), preferred_el...  28.3 us
    ppermute x4, starting transfers between devices, with_halo(): lax.ppermute(tail, axis, [(i, (i + 1) % count) for i in range(ends)])  21.6 us
    another operation x1, local copies, waits for them, and re-layouts, body(): jnp.stack([lax.dot_general(window, flat_grad, (((0,), (0,)), ((), ())), p...  10.3 us
    ppermute x2, waiting for transfers between devices, from_behind(): return lax.ppermute(array, axis, pairs)  8.87 us
    dot_general x27, matrix products, body(): lax.dot_general(back, conv_weight[t_off, h_off, w_off], (((1,), (1,)), ((...  8.85 us
    dot_general x27, matrix products, body(): jnp.dot(window, conv_weight[t_off, h_off, w_off], preferred_element_type=...  7.99 us
  transfers between devices with their start and end apart: 12, of which 8 were waited for; matrix products, arithmetic and copies ran while one was open for 4% of the time, Pallas kernels for 0%

commit v1 on v0

v1 whole, which is shorter than its diff:
```python
import jax
import jax.numpy as jnp
from jax import lax
from jax.experimental import pallas as pl
from jax.experimental.pallas import tpu as pltpu
from jax.sharding import PartitionSpec as P

EPSILON = 1e-06
MESH = pl.DeviceIdType.MESH
F32 = jnp.float32
BF16 = jnp.bfloat16
SLABS = 9
ROW = 18 * 16
PADDED = 6 * ROW
TICKS = 44


def dot(a, b):
    return jnp.dot(a, b, preferred_element_type=F32)


def wrap(value, count):
    return lax.rem(value + count, count)


def remote(src, dst, send, recv, device):
    return pltpu.make_async_remote_copy(
        src_ref=src, dst_ref=dst, send_sem=send, recv_sem=recv, device_id=device, device_id_type=MESH
    )


def normalise(cells, gain):
    values = cells.astype(F32)
    inverse = lax.rsqrt(jnp.mean(values * values, axis=-1, keepdims=True) + EPSILON)
    unit = values * inverse
    return values, inverse, unit, unit * gain


def kernel(
    scale,
    feat,
    gain,
    weight_hbm,
    cot,
    decoded,
    grad_feat,
    grad_weight,
    act,
    grd,
    act3,
    grd3,
    cot_t,
    weight,
    select,
    put_left,
    put_right,
    shift,
    edge,
    halo,
    mixed,
    back,
    part,
    pair,
    send1,
    recv1,
    mid,
    recv2,
    flat,
    recv3,
    total,
    weight_sem,
    halo_send,
    halo_recv,
    pair_sem,
    send1_sem,
    recv1_sem,
    send2_sem,
    recv2_sem,
    flat_sem,
    recv3_sem,
    total_send,
    total_recv,
):
    t = lax.axis_index("ta")
    ha = lax.axis_index("ha")
    wa = lax.axis_index("wa")
    core = lax.rem(ha, 2)
    x = (ha // 2) * 2 + wa // 4
    y = lax.rem(wa, 4)

    def at(z, xx, cc, yy):
        return (z, (xx // 2) * 2 + cc, lax.rem(xx, 2) * 4 + yy)

    def near(dt, dh, dw):
        return (wrap(t + dt, 8), wrap(ha + dh, 4), wrap(wa + dw, 8))

    partners = [near(0, 0, 1), near(0, 0, -1), near(0, 1, 0), near(0, -1, 0)]
    partners += [near(dt, dh, 0) for dt in (-1, 1) for dh in (-1, 1)]
    partners += [at(t, x, 1 - core, y)]
    partners += [at(t, wrap(x + k, 4), core, y) for k in (1, 2, 3)]
    partners += [at(t, x, core, wrap(y + k, 4)) for k in (1, 2, 3)]
    partners += [near(k, 0, 0) for k in range(1, 8)]
    barrier = pltpu.get_barrier_semaphore()
    for device in partners:
        pl.semaphore_signal(barrier, inc=1, device_id=device, device_id_type=MESH)

    load_weight = pltpu.make_async_copy(weight_hbm, weight, weight_sem)
    load_weight.start()

    @pl.loop(0, 16)
    def _(n):
        rows = pl.ds(pl.multiple_of(n * 64, 64), 64)
        normed = normalise(feat[rows, :], gain[...])[3]
        at_row = pl.multiple_of(((n // 4) * 18 + 1) * 16 + lax.rem(n, 4) * 64, 16)
        act[pl.ds(pl.multiple_of(at_row + 2 * ROW, 16), 64), :] = (normed * jax.nn.sigmoid(normed)).astype(BF16)
        grd[pl.ds(at_row, 64), :] = cot[rows, :]

    pl.semaphore_wait(barrier, len(partners))

    def block(ref, frame, frames, row, rows):
        return ref.at[pl.ds(frame, frames), pl.ds(row * 16, rows * 16), :]

    acts = act.reshape(6, ROW, 256)
    grds = grd.reshape(6, ROW, 256)
    first = []
    for n, (ref, dt, own, far) in enumerate(((acts, 1, 2, 0), (grds, -1, 0, 4))):
        edge_frame = 4 if dt == 1 else 0
        moves = [
            (near(dt, 0, 0), (edge_frame, 2, 1, 16), (far, 2, 1, 16)),
            (near(0, 1, 0), (own, 4, 16, 1), (own, 4, 0, 1)),
            (near(0, -1, 0), (own, 4, 1, 1), (own, 4, 17, 1)),
            (near(dt, 1, 0), (edge_frame, 2, 16, 1), (far, 2, 0, 1)),
            (near(dt, -1, 0), (edge_frame, 2, 1, 1), (far, 2, 17, 1)),
        ]
        first.append(
            [
                remote(block(ref, *src), block(ref, *dst), halo_send.at[n, m], halo_recv.at[n, m], device)
                for m, (device, src, dst) in enumerate(moves)
            ]
        )
    for copies in first:
        for copy in copies:
            copy.start()

    for n in range(4):
        cot_t[:, n * 256 : (n + 1) * 256] = cot[n * 256 : (n + 1) * 256, :].T

    def ones(condition):
        return jnp.where(condition, 1.0, 0.0).astype(BF16)

    cell = lax.broadcasted_iota(jnp.int32, (112, PADDED), 1)
    line = lax.broadcasted_iota(jnp.int32, (112, PADDED), 0) * 16
    select[0] = ones(cell == line + 15)
    select[1] = ones(cell == line)
    cell = lax.broadcasted_iota(jnp.int32, (PADDED, 112), 0)
    line = lax.broadcasted_iota(jnp.int32, (PADDED, 112), 1) * 16
    put_left[...] = ones(cell == line)
    put_right[...] = ones(cell == line + 15)
    cell = lax.broadcasted_iota(jnp.int32, (ROW, ROW), 0)
    other = lax.broadcasted_iota(jnp.int32, (ROW, ROW), 1)
    column = cell & 15
    shift[0] = ones((cell == other + 1) & (column != 0))
    shift[1] = ones((cell == other - 1) & (column != 15))

    second = []
    for n, (ref, refs, at_edge, edges) in enumerate(((act, acts, t == 0, (0, 1)), (grd, grds, t == 7, (4, 5)))):
        for copy in first[n]:
            copy.wait_recv()
        for copy in first[n]:
            copy.wait_send()

        @pl.when(at_edge)
        def _():
            for frame in edges:
                refs[frame] = jnp.zeros((ROW, 256), BF16)

        @pl.when(ha == 0)
        def _():
            for frame in range(6):
                refs[frame, 0:16, :] = jnp.zeros((16, 256), BF16)

        @pl.when(ha == 3)
        def _():
            for frame in range(6):
                refs[frame, 17 * 16 : ROW, :] = jnp.zeros((16, 256), BF16)

        copies = []
        for side in range(2):
            edge[n, side] = dot(select[side], ref[...]).astype(BF16)
            copy = remote(
                edge.at[n, side],
                halo.at[n, side],
                halo_send.at[n, 5 + side],
                halo_recv.at[n, 5 + side],
                near(0, 0, 1 if side == 0 else -1),
            )
            copy.start()
            copies.append(copy)
        second.append(copies)

    for n, (ref, wide) in enumerate(((act, act3), (grd, grd3))):
        wide[:, 256:512] = ref[...]
        for copy in second[n]:
            copy.wait_recv()

        @pl.when(wa == 0)
        def _():
            halo[n, 0] = jnp.zeros((112, 256), BF16)

        @pl.when(wa == 7)
        def _():
            halo[n, 1] = jnp.zeros((112, 256), BF16)

        for side, put, lanes in ((0, put_left, 0), (1, put_right, 512)):

            @pl.loop(0, 6)
            def _(frame):
                rows = pl.ds(pl.multiple_of(frame * ROW, 16), ROW)
                moved = dot(shift[side], ref[rows, :]) + dot(put[rows, :], halo[n, side])
                wide[rows, lanes : lanes + 256] = moved.astype(BF16)

        for copy in second[n]:
            copy.wait_send()

    load_weight.wait()
    mixed[...] = jnp.zeros_like(mixed)
    back[...] = jnp.zeros_like(back)

    def to_pair(s):
        return remote(
            part.at[s, :, 1 - core], pair.at[s], pair_sem.at[0, s], pair_sem.at[1, s], at(t, x, 1 - core, y)
        )

    def along(half, k):
        return at(t, wrap(x + k, 4), core, y) if half == 0 else at(t, x, core, wrap(y + k, 4))

    def copy1(s, half, k):
        slot = wrap((x if half == 0 else y) + k, 4)
        return remote(
            send1.at[s, half, slot],
            recv1.at[s, half, k - 1],
            send1_sem.at[s, half, k - 1],
            recv1_sem.at[s, half, k - 1],
            along(half, k),
        )

    def copy2(s, half, k):
        slot = wrap((y if half == 0 else x) + k, 4)
        return remote(
            mid.at[s, half, slot],
            recv2.at[s, half, k - 1],
            send2_sem.at[s, half, k - 1],
            recv2_sem.at[s, half, k - 1],
            along(1 - half, k),
        )

    def stage_gradient(s):
        i, j = s // 3, lax.rem(s, 3)
        acc = None
        for n in range(4):
            rows = pl.ds(pl.multiple_of((n + i) * ROW + j * 16, 16), 256)
            term = dot(cot_t[:, n * 256 : (n + 1) * 256], act3[rows, :])
            acc = term if acc is None else acc + term
        part[s] = acc.reshape(2, 2, 64, 768)
        to_pair(s).start()

    def stage_first(s):
        to_pair(s).wait_recv()
        for n in range(2):
            pair[s, n] = pair[s, n] + part[s, n, core]
        for d in range(4):
            n, r = d // 2, (d % 2) * 32
            send1[s, 0, d] = pair[s, n, r : r + 32, 0:384].astype(BF16)
            rows = [pair[s, e // 2, (e % 2) * 32 + d * 8 : (e % 2) * 32 + d * 8 + 8, 384:768] for e in range(4)]
            send1[s, 1, d] = jnp.concatenate(rows, axis=0).astype(BF16)
        for k in (2, 1, 3):
            for half in range(2):
                copy1(s, half, k).start()

    def stage_second(s):
        for half in range(2):
            for k in (1, 2, 3):
                copy1(s, half, k).wait_recv()
        own = pair[s, x // 2, pl.ds(pl.multiple_of(lax.rem(x, 2) * 32, 32), 32), 0:384]
        for k in range(3):
            own = own + recv1[s, 0, k].astype(F32)
        mid[s, 0] = own.reshape(4, 8, 384)
        rows = [
            pair[s, e // 2, pl.ds(pl.multiple_of((e % 2) * 32 + y * 8, 8), 8), 384:768] for e in range(4)
        ]
        own = jnp.concatenate(rows, axis=0)
        for k in range(3):
            own = own + recv1[s, 1, k].astype(F32)
        mid[s, 1] = own.reshape(4, 8, 384)
        for k in (2, 1, 3):
            for half in range(2):
                copy2(s, half, k).start()

    def owner_of(s):
        return lax.rem(s, 8)

    def to_owner(s):
        k = wrap(t - owner_of(s) - 1, 8)
        return remote(
            flat.at[s], recv3.at[s // 8, k], flat_sem.at[s], recv3_sem.at[s // 8, k], (owner_of(s), ha, wa)
        )

    def from_owner(s, k):
        return remote(
            total.at[s],
            total.at[s],
            total_send.at[s // 8, k - 1],
            total_recv.at[s],
            (wrap(t + k, 8), ha, wa),
        )

    def stage_third(s):
        for half in range(2):
            for k in (1, 2, 3):
                copy2(s, half, k).wait_recv()
        for half, slot in ((0, y), (1, x)):
            own = mid[s, half, slot]
            for k in range(3):
                own = own + recv2[s, half, k]
            flat[s, :, half * 384 : half * 384 + 384] = own

        @pl.when(t != owner_of(s))
        def _():
            to_owner(s).start()

    def stage_owner(s):
        @pl.when(t == owner_of(s))
        def _():
            for k in range(7):
                remote(
                    flat.at[s], recv3.at[s // 8, k], flat_sem.at[s], recv3_sem.at[s // 8, k], near(1, 0, 0)
                ).wait_recv()
            own = flat[s]
            for k in range(7):
                own = own + recv3[s // 8, k]
            own = own * scale
            for k in range(3):
                total[s, k] = own[:, k * 256 : k * 256 + 256]
            for k in (4, 3, 5, 2, 6, 1, 7):
                from_owner(s, k).start()

    def stage_mixed(s):
        i, j = s // 3, lax.rem(s, 3)
        for n in range(4):
            rows = pl.ds(pl.multiple_of((n + i) * ROW + j * 16, 16), 256)
            mixed[n * 256 : n * 256 + 256, :] += dot(act3[rows, :], weight[s])

    def stage_back(s):
        i, j = s // 3, lax.rem(s, 3)
        for n in range(4):
            rows = pl.ds(pl.multiple_of((n + 2 - i) * ROW + (2 - j) * 16, 16), 256)
            acc = None
            for k in range(3):
                term = lax.dot_general(
                    grd3[rows, (2 - k) * 256 : (3 - k) * 256],
                    weight[s, k * 256 : k * 256 + 256, :],
                    (((1,), (1,)), ((), ())),
                    preferred_element_type=F32,
                )
                acc = term if acc is None else acc + term
            back[n * 256 : n * 256 + 256, :] += acc

    plan = (
        (stage_gradient, 0, 1),
        (stage_first, 2, 1),
        (stage_second, 8, 2),
        (stage_third, 13, 2),
        (stage_owner, 19, 2),
        (stage_mixed, 9, 1),
        (stage_back, 18, 1),
    )

    @pl.loop(0, TICKS)
    def _(tick):
        for stage, begin, step in plan:
            s = (tick - begin) // step

            @pl.when((tick >= begin) & (s < SLABS) & (lax.rem(tick - begin + 64, step) == 0))
            def _():
                stage(s)

    @pl.loop(0, 16)
    def _(n):
        rows = pl.ds(pl.multiple_of(n * 64, 64), 64)
        values, inverse, unit, normed = normalise(feat[rows, :], gain[...])
        decoded[rows, :] = (values + mixed[rows, :]).astype(BF16)
        logistic = jax.nn.sigmoid(normed)
        grad_unit = back[rows, :] * logistic * (1.0 + normed * (1.0 - logistic)) * gain[...]
        grad = inverse * (grad_unit - unit * jnp.mean(grad_unit * unit, axis=-1, keepdims=True))
        grad_feat[rows, :] = (cot[rows, :].astype(F32) + grad).astype(BF16)

    @pl.loop(0, SLABS)
    def _(s):
        to_pair(s).wait_send()
        for half in range(2):
            for k in (1, 2, 3):
                copy1(s, half, k).wait_send()
                copy2(s, half, k).wait_send()

        @pl.when(t != owner_of(s))
        def _():
            to_owner(s).wait_send()
            from_owner(s, 1).wait_recv()

        @pl.when(t == owner_of(s))
        def _():
            for k in range(1, 8):
                from_owner(s, k).wait_send()

        for k in range(3):
            grad_weight[s * 3 + k] = total[s, k]


def body(features, norm_gain, conv_weight, cotangent):
    frames, height, width, channels = features.shape
    cells = frames * height * width
    owners = lax.axis_size("ha") * lax.axis_size("wa")
    voxels = cells * owners * lax.axis_size("ta")
    vmem = pl.BlockSpec(memory_space=pltpu.VMEM)
    dma = pltpu.SemaphoreType.DMA

    def run(*refs):
        kernel(float(voxels) ** (-0.5), *refs)

    decoded, grad_features, grad_weight = pl.pallas_call(
        run,
        out_shape=(
            jax.ShapeDtypeStruct((cells, channels), BF16),
            jax.ShapeDtypeStruct((cells, channels), BF16),
            jax.ShapeDtypeStruct((27, channels // owners, channels), F32),
        ),
        in_specs=[vmem, vmem, pl.BlockSpec(memory_space=pl.ANY), vmem],
        out_specs=(vmem, vmem, vmem),
        scratch_shapes=[
            pltpu.VMEM((PADDED, 256), BF16),
            pltpu.VMEM((PADDED, 256), BF16),
            pltpu.VMEM((PADDED, 768), BF16),
            pltpu.VMEM((PADDED, 768), BF16),
            pltpu.VMEM((256, 1024), BF16),
            pltpu.VMEM((SLABS, 768, 256), BF16),
            pltpu.VMEM((2, 112, PADDED), BF16),
            pltpu.VMEM((PADDED, 112), BF16),
            pltpu.VMEM((PADDED, 112), BF16),
            pltpu.VMEM((2, ROW, ROW), BF16),
            pltpu.VMEM((2, 2, 112, 256), BF16),
            pltpu.VMEM((2, 2, 112, 256), BF16),
            pltpu.VMEM((1024, 256), F32),
            pltpu.VMEM((1024, 256), F32),
            pltpu.VMEM((SLABS, 2, 2, 64, 768), F32),
            pltpu.VMEM((SLABS, 2, 64, 768), F32),
            pltpu.VMEM((SLABS, 2, 4, 32, 384), BF16),
            pltpu.VMEM((SLABS, 2, 3, 32, 384), BF16),
            pltpu.VMEM((SLABS, 2, 4, 8, 384), F32),
            pltpu.VMEM((SLABS, 2, 3, 8, 384), F32),
            pltpu.VMEM((SLABS, 8, 768), F32),
            pltpu.VMEM((2, 7, 8, 768), F32),
            pltpu.VMEM((SLABS, 3, 8, 256), F32),
            dma,
            dma((2, 7)),
            dma((2, 7)),
            dma((2, SLABS)),
            dma((SLABS, 2, 3)),
            dma((SLABS, 2, 3)),
            dma((SLABS, 2, 3)),
            dma((SLABS, 2, 3)),
            dma((SLABS,)),
            dma((2, 7)),
            dma((2, 7)),
            dma((SLABS,)),
        ],
        compiler_params=pltpu.CompilerParams(
            collective_id=0, has_side_effects=True, vmem_limit_bytes=60 << 20
        ),
    )(
        features.reshape(cells, channels),
        norm_gain.reshape(1, channels),
        conv_weight.reshape(9, 3 * channels, channels),
        cotangent.reshape(cells, channels),
    )
    grad_weight = grad_weight.reshape(3, 3, 3, channels // owners, channels).transpose(0, 1, 2, 4, 3)
    return decoded.reshape(features.shape), grad_features.reshape(features.shape), grad_weight


def solution(mesh):
    placed = (P("ta", "ha", "wa", None), P(), P(), P("ta", "ha", "wa", None))
    return jax.shard_map(
        body,
        mesh=mesh,
        in_specs=placed,
        out_specs=(
            P("ta", "ha", "wa", None),
            P("ta", "ha", "wa", None),
            P(None, None, None, None, ("ha", "wa")),
        ),
        check_vma=False,
    )
```

time: 365 us -> 82 us (0.22); the launches traced: 360 us -> 81.7 us
  waiting for transfers between devices: 237 us -> 0 us
  Pallas kernels: 0 us -> 75.7 us
  matrix products: 45.1 us -> 0 us
  starting transfers between devices: 33.2 us -> 0 us
  local copies, waits for them, and re-layouts: 21.4 us -> 5.37 us
  between operations: 14.7 us -> 0.64 us
  other arithmetic: 9.12 us -> 0 us
    reduce_scatter x1 -> x0, waiting for transfers between devices: 148 us -> none  [body(): lax.psum_scatter(weight_taps, ('ha', 'wa'), scatter_dimension=2, tiled=True)]
    pallas_call x0 -> x1, Pallas kernels: none -> 75.7 us  [body(): pl.pallas_call(run, out_shape=(jax.ShapeDtypeStruct((cells, channels), BF...]
    psum x1 -> x0, waiting for transfers between devices: 71 us -> none  [body(): summed = lax.psum(shared, 'ta')]
    dot_general x81 -> x0, matrix products: 45.1 us -> none  [the longest x27 28.3 us: body(): lax.dot_general(window, flat_grad, (((0,), (0,)), ((), ())), preferred_el...]
    ppermute x10 -> x0, starting transfers between devices: 32.9 us -> none  [the longest x4 21.6 us: with_halo(): lax.ppermute(tail, axis, [(i, (i + 1) % count) for i in range(ends)])]
    ppermute x10 -> x0, waiting for transfers between devices: 17.3 us -> none  [the longest x2 8.87 us: from_behind(): return lax.ppermute(array, axis, pairs)]
    another operation x1 -> x0, local copies, waits for them, and re-layouts: 10.3 us -> none  [body(): jnp.stack([lax.dot_general(window, flat_grad, (((0,), (0,)), ((), ())), p...]
    slice x8 -> x0, local copies, waits for them, and re-layouts: 5.9 us -> none  [the longest x1 3.32 us: body(): grad_padded[2 - t_off:2 - t_off + frames, 2 - h_off:2 - h_off + height, 2...]
  transfers between devices with their start and end apart: 12 -> 0, of which waited for: 8 -> 0; matrix products, arithmetic and copies ran while one was open for 4% -> 0% of each run, Pallas kernels for 0% -> 0%
where the time goes in v1:
time: 82 us; the launch traced here: 81.7 us
  Pallas kernels  75.7 us (92%)
  local copies, waits for them, and re-layouts  5.37 us (7%)
    pallas_call x1, Pallas kernels, body(): pl.pallas_call(run, out_shape=(jax.ShapeDtypeStruct((cells, channels), BF...  75.7 us
    unnamed x3, local copies, waits for them, and re-layouts  5.37 us

profile of v1, /device:TPU:1, one launch (start us, length us, event | category | flops | bytes accessed | tf_op | source)
XLA Modules:
  0.0 81.7 jit_solution(16162733278802972971)
XLA Ops:
  0.6 75.7 %shard_map.67 = (bf16[1024,256]{1,0:T(8,128)(2,1)}, bf16[1024,256]{1,0:T(8,128)(2,1)}, f32[27,8,256]{2,1,0:T(8,128)}) custom-call(bf16[1024,256]{1,0:T(8,128)(2,1)} %bitcast.10, f32[1,256]{1,0:T(1,128)} %bitcast.15, bf16[9,768,256]{2,1,0:T(8,128)(2,1)} %bitcast.9, bf16[1024,256]{1,0:T(8,128)(2,1)} %bitcast.11), custom_call_target="tpu_custom_call" | custom-call | tf_op jit(solution)/shard_map/pallas_call | solution.py:430
  76.4 1.9 %copy.10 = bf16[4,16,16,256]{3,2,1,0:T(8,128)(2,1)} copy(bf16[4,16,16,256]{3,2,1,0:T(8,128)(2,1)} %bitcast.13) | data formatting | bytes 1048576
  78.2 1.9 %copy.11 = bf16[4,16,16,256]{3,2,1,0:T(8,128)(2,1)} copy(bf16[4,16,16,256]{3,2,1,0:T(8,128)(2,1)} %bitcast.12) | data formatting | bytes 1048576
  80.1 1.6 %copy.12 = f32[3,3,3,256,8]{3,4,2,1,0:T(8,128)} copy(f32[3,3,3,256,8]{3,4,2,1,0:T(8,128)} %bitcast.14) | data formatting | bytes 442368

commit v2 on v1

--- a/solution.py
+++ b/solution.py
@@ -12,7 +12,7 @@
 SLABS = 9
 ROW = 18 * 16
 PADDED = 6 * ROW
-TICKS = 44
+TICKS = 38
 
 
 def dot(a, b):
@@ -38,13 +38,15 @@
 
 def kernel(
     scale,
-    feat,
+    feat_hbm,
     gain,
     weight_hbm,
-    cot,
+    cot_hbm,
     decoded,
     grad_feat,
     grad_weight,
+    feat,
+    cot,
     act,
     grd,
     act3,
@@ -52,11 +54,11 @@
     cot_t,
     weight,
     select,
-    put_left,
-    put_right,
+    put,
     shift,
     edge,
     halo,
+    halo_t,
     mixed,
     back,
     part,
@@ -68,7 +70,7 @@
     flat,
     recv3,
     total,
-    weight_sem,
+    load_sem,
     halo_send,
     halo_recv,
     pair_sem,
@@ -94,8 +96,7 @@
     def near(dt, dh, dw):
         return (wrap(t + dt, 8), wrap(ha + dh, 4), wrap(wa + dw, 8))
 
-    partners = [near(0, 0, 1), near(0, 0, -1), near(0, 1, 0), near(0, -1, 0)]
-    partners += [near(dt, dh, 0) for dt in (-1, 1) for dh in (-1, 1)]
+    partners = [near(0, dh, dw) for dh in (-1, 0, 1) for dw in (-1, 0, 1) if (dh, dw) != (0, 0)]
     partners += [at(t, x, 1 - core, y)]
     partners += [at(t, wrap(x + k, 4), core, y) for k in (1, 2, 3)]
     partners += [at(t, x, core, wrap(y + k, 4)) for k in (1, 2, 3)]
@@ -104,127 +105,153 @@
     for device in partners:
         pl.semaphore_signal(barrier, inc=1, device_id=device, device_id_type=MESH)
 
-    load_weight = pltpu.make_async_copy(weight_hbm, weight, weight_sem)
-    load_weight.start()
-
-    @pl.loop(0, 16)
-    def _(n):
-        rows = pl.ds(pl.multiple_of(n * 64, 64), 64)
-        normed = normalise(feat[rows, :], gain[...])[3]
-        at_row = pl.multiple_of(((n // 4) * 18 + 1) * 16 + lax.rem(n, 4) * 64, 16)
-        act[pl.ds(pl.multiple_of(at_row + 2 * ROW, 16), 64), :] = (normed * jax.nn.sigmoid(normed)).astype(BF16)
-        grd[pl.ds(at_row, 64), :] = cot[rows, :]
-
-    pl.semaphore_wait(barrier, len(partners))
-
-    def block(ref, frame, frames, row, rows):
-        return ref.at[pl.ds(frame, frames), pl.ds(row * 16, rows * 16), :]
-
-    acts = act.reshape(6, ROW, 256)
-    grds = grd.reshape(6, ROW, 256)
-    first = []
-    for n, (ref, dt, own, far) in enumerate(((acts, 1, 2, 0), (grds, -1, 0, 4))):
-        edge_frame = 4 if dt == 1 else 0
-        moves = [
-            (near(dt, 0, 0), (edge_frame, 2, 1, 16), (far, 2, 1, 16)),
-            (near(0, 1, 0), (own, 4, 16, 1), (own, 4, 0, 1)),
-            (near(0, -1, 0), (own, 4, 1, 1), (own, 4, 17, 1)),
-            (near(dt, 1, 0), (edge_frame, 2, 16, 1), (far, 2, 0, 1)),
-            (near(dt, -1, 0), (edge_frame, 2, 1, 1), (far, 2, 17, 1)),
-        ]
-        first.append(
-            [
-                remote(block(ref, *src), block(ref, *dst), halo_send.at[n, m], halo_recv.at[n, m], device)
-                for m, (device, src, dst) in enumerate(moves)
-            ]
-        )
-    for copies in first:
-        for copy in copies:
-            copy.start()
-
-    for n in range(4):
-        cot_t[:, n * 256 : (n + 1) * 256] = cot[n * 256 : (n + 1) * 256, :].T
+    loads = [
+        pltpu.make_async_copy(far, here, load_sem.at[n])
+        for n, (far, here) in enumerate(((feat_hbm, feat), (cot_hbm, cot), (weight_hbm, weight)))
+    ]
+    for load in loads:
+        load.start()
 
     def ones(condition):
         return jnp.where(condition, 1.0, 0.0).astype(BF16)
 
-    cell = lax.broadcasted_iota(jnp.int32, (112, PADDED), 1)
-    line = lax.broadcasted_iota(jnp.int32, (112, PADDED), 0) * 16
-    select[0] = ones(cell == line + 15)
-    select[1] = ones(cell == line)
-    cell = lax.broadcasted_iota(jnp.int32, (PADDED, 112), 0)
-    line = lax.broadcasted_iota(jnp.int32, (PADDED, 112), 1) * 16
-    put_left[...] = ones(cell == line)
-    put_right[...] = ones(cell == line + 15)
+    line = lax.broadcasted_iota(jnp.int32, (96, 1024), 0)
+    cell = lax.broadcasted_iota(jnp.int32, (96, 1024), 1)
+    first_column = jnp.where(line < 64, line * 16, (line & 15) * 256 + jnp.where(line < 80, 240, 0))
+    usable = (line < 64) | ((line & 15) < 4)
+    select[0] = ones(usable & (cell == first_column + 15))
+    select[1] = ones(usable & (cell == first_column))
+    for n in range(4):
+        line = lax.broadcasted_iota(jnp.int32, (ROW, 96), 1)
+        cell = lax.broadcasted_iota(jnp.int32, (ROW, 96), 0)
+        row = jnp.where(line < 64, (line & 15) + 1, jnp.where(line < 80, 0, 17))
+        frame = jnp.where(line < 64, line // 16, line & 15)
+        put[0, n] = ones((frame == n) & (cell == row * 16))
+        put[1, n] = ones((frame == n) & (cell == row * 16 + 15))
     cell = lax.broadcasted_iota(jnp.int32, (ROW, ROW), 0)
     other = lax.broadcasted_iota(jnp.int32, (ROW, ROW), 1)
     column = cell & 15
     shift[0] = ones((cell == other + 1) & (column != 0))
     shift[1] = ones((cell == other - 1) & (column != 15))
 
-    second = []
-    for n, (ref, refs, at_edge, edges) in enumerate(((act, acts, t == 0, (0, 1)), (grd, grds, t == 7, (4, 5)))):
+    loads[0].wait()
+
+    @pl.loop(0, 16)
+    def _(n):
+        rows = pl.ds(pl.multiple_of(n * 64, 64), 64)
+        normed = normalise(feat[rows, :], gain[...])[3]
+        act[2 + n // 4, pl.ds(pl.multiple_of(lax.rem(n, 4) * 64 + 16, 16), 64), :] = (
+            normed * jax.nn.sigmoid(normed)
+        ).astype(BF16)
+
+    loads[1].wait()
+    for n in range(4):
+        grd[n, 16:272, :] = cot[n * 256 : n * 256 + 256, :]
+    for n, (ref, own) in enumerate(((act, 2), (grd, 0))):
+        for side in range(2):
+            acc = None
+            for f in range(4):
+                term = dot(select[side, :, f * 256 : f * 256 + 256], ref[own + f, 16:272, :])
+                acc = term if acc is None else acc + term
+            edge[n, side] = acc.astype(BF16)
+
+    pl.semaphore_wait(barrier, len(partners))
+
+    def rows_of(ref, frame, frames, row, rows):
+        return ref.at[pl.ds(frame, frames), pl.ds(row * 16, rows * 16), :]
+
+    first = []
+    early = []
+    late = []
+    for n, (ref, dt, own, ends) in enumerate(((act, 1, 2, ((5, 1), (4, 0))), (grd, -1, 0, ((0, 4), (1, 5))))):
+        at_sem = iter(range(13))
+
+        def move(source, target, device):
+            m = next(at_sem)
+            return remote(source, target, halo_send.at[n, m], halo_recv.at[n, m], device)
+
+        moves = [
+            move(rows_of(ref, own, 4, 16, 1), rows_of(ref, own, 4, 0, 1), near(0, 1, 0)),
+            move(rows_of(ref, own, 4, 1, 1), rows_of(ref, own, 4, 17, 1), near(0, -1, 0)),
+        ]
+        for side, dw in ((0, 1), (1, -1)):
+            for begin, count, dh in ((0, 64, 0), (64, 16, 1), (80, 16, -1)):
+                lines = pl.ds(begin, count)
+                moves.append(move(edge.at[n, side, lines], halo.at[n, side, lines], near(0, dh, dw)))
+        first.append(moves)
+        early.append([move(rows_of(ref, a, 1, 1, 16), rows_of(ref, b, 1, 1, 16), near(dt, 0, 0)) for a, b in ends])
+        (a0, b0), (a1, b1) = ends
+        a, b = min(a0, a1), min(b0, b1)
+        late.append(
+            [move(rows_of(ref, a, 2, row, 1), rows_of(ref, b, 2, row, 1), near(dt, 0, 0)) for row in (0, 17)]
+            + [move(halo.at[n], halo_t.at[n], near(dt, 0, 0))]
+        )
+    for group in (first[0], early[0], first[1], early[1]):
+        for copy in group:
+            copy.start()
+
+    for n in range(4):
+        cot_t[:, n * 256 : (n + 1) * 256] = cot[n * 256 : (n + 1) * 256, :].T
+    mixed[...] = jnp.zeros_like(mixed)
+    back[...] = jnp.zeros_like(back)
+    loads[2].wait()
+
+    def take_first(n, ref, own):
         for copy in first[n]:
             copy.wait_recv()
         for copy in first[n]:
             copy.wait_send()
 
-        @pl.when(at_edge)
-        def _():
-            for frame in edges:
-                refs[frame] = jnp.zeros((ROW, 256), BF16)
-
         @pl.when(ha == 0)
         def _():
-            for frame in range(6):
-                refs[frame, 0:16, :] = jnp.zeros((16, 256), BF16)
+            for frame in range(4):
+                ref[own + frame, 0:16, :] = jnp.zeros((16, 256), BF16)
+            for side in range(2):
+                halo[n, side, 64:80] = jnp.zeros((16, 256), BF16)
 
         @pl.when(ha == 3)
         def _():
-            for frame in range(6):
-                refs[frame, 17 * 16 : ROW, :] = jnp.zeros((16, 256), BF16)
-
-        copies = []
-        for side in range(2):
-            edge[n, side] = dot(select[side], ref[...]).astype(BF16)
-            copy = remote(
-                edge.at[n, side],
-                halo.at[n, side],
-                halo_send.at[n, 5 + side],
-                halo_recv.at[n, 5 + side],
-                near(0, 0, 1 if side == 0 else -1),
-            )
+            for frame in range(4):
+                ref[own + frame, 272:288, :] = jnp.zeros((16, 256), BF16)
+            for side in range(2):
+                halo[n, side, 80:96] = jnp.zeros((16, 256), BF16)
+
+        @pl.when(wa == 0)
+        def _():
+            halo[n, 0] = jnp.zeros((96, 256), BF16)
+
+        @pl.when(wa == 7)
+        def _():
+            halo[n, 1] = jnp.zeros((96, 256), BF16)
+
+        for copy in late[n]:
             copy.start()
-            copies.append(copy)
-        second.append(copies)
-
-    for n, (ref, wide) in enumerate(((act, act3), (grd, grd3))):
-        wide[:, 256:512] = ref[...]
-        for copy in second[n]:
+
+    def take_late(n, ref, far, at_end):
+        for copy in early[n] + late[n]:
             copy.wait_recv()
-
-        @pl.when(wa == 0)
-        def _():
-            halo[n, 0] = jnp.zeros((112, 256), BF16)
-
-        @pl.when(wa == 7)
-        def _():
-            halo[n, 1] = jnp.zeros((112, 256), BF16)
-
-        for side, put, lanes in ((0, put_left, 0), (1, put_right, 512)):
-
-            @pl.loop(0, 6)
-            def _(frame):
-                rows = pl.ds(pl.multiple_of(frame * ROW, 16), ROW)
-                moved = dot(shift[side], ref[rows, :]) + dot(put[rows, :], halo[n, side])
-                wide[rows, lanes : lanes + 256] = moved.astype(BF16)
-
-        for copy in second[n]:
+        for copy in early[n] + late[n]:
             copy.wait_send()
 
-    load_weight.wait()
-    mixed[...] = jnp.zeros_like(mixed)
-    back[...] = jnp.zeros_like(back)
+        @pl.when(at_end)
+        def _():
+            for frame in (far, far + 1):
+                ref[frame] = jnp.zeros((ROW, 256), BF16)
+            for side in range(2):
+                halo_t[n, side] = jnp.zeros((96, 256), BF16)
+
+    def widen(n, ref, wide, frame, own, borders):
+        rows = pl.ds(pl.multiple_of(frame * ROW, 16), ROW)
+        wide[rows, 256:512] = ref[frame]
+        for side, lanes in ((0, 0), (1, 512)):
+            moved = dot(shift[side], ref[frame]) + dot(put[side, own], borders[n, side])
+            wide[rows, lanes : lanes + 256] = moved.astype(BF16)
+
+    take_first(0, act, 2)
+
+    @pl.loop(0, 4)
+    def _(frame):
+        widen(0, act, act3, frame + 2, frame, halo)
 
     def to_pair(s):
         return remote(
@@ -255,7 +282,7 @@
         )
 
     def stage_gradient(s):
-        i, j = s // 3, lax.rem(s, 3)
+        i, j = 2 - s // 3, lax.rem(s, 3)
         acc = None
         for n in range(4):
             rows = pl.ds(pl.multiple_of((n + i) * ROW + j * 16, 16), 256)
@@ -365,34 +392,58 @@
                 acc = term if acc is None else acc + term
             back[n * 256 : n * 256 + 256, :] += acc
 
+    def stage_act(_):
+        take_late(0, act, 0, t == 0)
+        for frame in range(2):
+            widen(0, act, act3, frame, frame + 2, halo_t)
+        take_first(1, grd, 0)
+
+    def stage_cot(frame):
+        widen(1, grd, grd3, frame, frame, halo)
+
+    def stage_cot_late(_):
+        take_late(1, grd, 4, t == 7)
+        for frame in range(2):
+            widen(1, grd, grd3, frame + 4, frame, halo_t)
+
+    def stage_decoded(n):
+        for m in range(4):
+            rows = pl.ds(pl.multiple_of(n * 256 + m * 64, 64), 64)
+            decoded[rows, :] = (feat[rows, :].astype(F32) + mixed[rows, :]).astype(BF16)
+
+    def stage_grad(n):
+        @pl.loop(0, 4)
+        def _(m):
+            rows = pl.ds(pl.multiple_of(n * 256 + m * 64, 64), 64)
+            _, inverse, unit, normed = normalise(feat[rows, :], gain[...])
+            logistic = jax.nn.sigmoid(normed)
+            grad_unit = back[rows, :] * logistic * (1.0 + normed * (1.0 - logistic)) * gain[...]
+            grad = inverse * (grad_unit - unit * jnp.mean(grad_unit * unit, axis=-1, keepdims=True))
+            grad_feat[rows, :] = (cot[rows, :].astype(F32) + grad).astype(BF16)
+
     plan = (
-        (stage_gradient, 0, 1),
-        (stage_first, 2, 1),
-        (stage_second, 8, 2),
-        (stage_third, 13, 2),
-        (stage_owner, 19, 2),
-        (stage_mixed, 9, 1),
-        (stage_back, 18, 1),
+        (stage_act, 3, 1, 1),
+        (stage_gradient, 0, 1, SLABS),
+        (stage_first, 2, 1, SLABS),
+        (stage_second, 8, 2, SLABS),
+        (stage_third, 13, 2, SLABS),
+        (stage_owner, 20, 2, SLABS),
+        (stage_mixed, 9, 1, SLABS),
+        (stage_cot, 9, 1, 4),
+        (stage_cot_late, 14, 1, 1),
+        (stage_back, 18, 1, SLABS),
+        (stage_decoded, 19, 2, 4),
+        (stage_grad, 27, 1, 4),
     )
 
     @pl.loop(0, TICKS)
     def _(tick):
-        for stage, begin, step in plan:
+        for stage, begin, step, count in plan:
             s = (tick - begin) // step
 
-            @pl.when((tick >= begin) & (s < SLABS) & (lax.rem(tick - begin + 64, step) == 0))
+            @pl.when((tick >= begin) & (tick < begin + step * count) & (lax.rem(tick - begin + 64, step) == 0))
             def _():
                 stage(s)
-
-    @pl.loop(0, 16)
-    def _(n):
-        rows = pl.ds(pl.multiple_of(n * 64, 64), 64)
-        values, inverse, unit, normed = normalise(feat[rows, :], gain[...])
-        decoded[rows, :] = (values + mixed[rows, :]).astype(BF16)
-        logistic = jax.nn.sigmoid(normed)
-        grad_unit = back[rows, :] * logistic * (1.0 + normed * (1.0 - logistic)) * gain[...]
-        grad = inverse * (grad_unit - unit * jnp.mean(grad_unit * unit, axis=-1, keepdims=True))
-        grad_feat[rows, :] = (cot[rows, :].astype(F32) + grad).astype(BF16)
 
     @pl.loop(0, SLABS)
     def _(s):
@@ -413,7 +464,15 @@
                 from_owner(s, k).wait_send()
 
         for k in range(3):
-            grad_weight[s * 3 + k] = total[s, k]
+            grad_weight[(2 - s // 3) * 9 + lax.rem(s, 3) * 3 + k] = total[s, k]
+
+
+def finish(*refs):
+    copies = [pltpu.make_async_copy(refs[n], refs[n + 3], refs[6].at[n]) for n in range(3)]
+    for copy in copies:
+        copy.start()
+    for copy in copies:
+        copy.wait()
 
 
 def body(features, norm_gain, conv_weight, cotangent):
@@ -422,33 +481,38 @@
     owners = lax.axis_size("ha") * lax.axis_size("wa")
     voxels = cells * owners * lax.axis_size("ta")
     vmem = pl.BlockSpec(memory_space=pltpu.VMEM)
+    hbm = pl.BlockSpec(memory_space=pltpu.HBM)
+    anywhere = pl.BlockSpec(memory_space=pl.ANY)
     dma = pltpu.SemaphoreType.DMA
 
     def run(*refs):
         kernel(float(voxels) ** (-0.5), *refs)
 
-    decoded, grad_features, grad_weight = pl.pallas_call(
+    results = (
+        jax.ShapeDtypeStruct((cells, channels), BF16),
+        jax.ShapeDtypeStruct((cells, channels), BF16),
+        jax.ShapeDtypeStruct((27, channels // owners, channels), F32),
+    )
+    held = pl.pallas_call(
         run,
-        out_shape=(
-            jax.ShapeDtypeStruct((cells, channels), BF16),
-            jax.ShapeDtypeStruct((cells, channels), BF16),
-            jax.ShapeDtypeStruct((27, channels // owners, channels), F32),
-        ),
-        in_specs=[vmem, vmem, pl.BlockSpec(memory_space=pl.ANY), vmem],
+        out_shape=results,
+        in_specs=[hbm, vmem, hbm, hbm],
         out_specs=(vmem, vmem, vmem),
         scratch_shapes=[
-            pltpu.VMEM((PADDED, 256), BF16),
-            pltpu.VMEM((PADDED, 256), BF16),
+            pltpu.VMEM((1024, 256), BF16),
+            pltpu.VMEM((1024, 256), BF16),
+            pltpu.VMEM((6, ROW, 256), BF16),
+            pltpu.VMEM((6, ROW, 256), BF16),
             pltpu.VMEM((PADDED, 768), BF16),
             pltpu.VMEM((PADDED, 768), BF16),
             pltpu.VMEM((256, 1024), BF16),
             pltpu.VMEM((SLABS, 768, 256), BF16),
-            pltpu.VMEM((2, 112, PADDED), BF16),
-            pltpu.VMEM((PADDED, 112), BF16),
-            pltpu.VMEM((PADDED, 112), BF16),
+            pltpu.VMEM((2, 96, 1024), BF16),
+            pltpu.VMEM((2, 4, ROW, 96), BF16),
             pltpu.VMEM((2, ROW, ROW), BF16),
-            pltpu.VMEM((2, 2, 112, 256), BF16),
-            pltpu.VMEM((2, 2, 112, 256), BF16),
+            pltpu.VMEM((2, 2, 96, 256), BF16),
+            pltpu.VMEM((2, 2, 96, 256), BF16),
+            pltpu.VMEM((2, 2, 96, 256), BF16),
             pltpu.VMEM((1024, 256), F32),
             pltpu.VMEM((1024, 256), F32),
             pltpu.VMEM((SLABS, 2, 2, 64, 768), F32),
@@ -460,9 +524,9 @@
             pltpu.VMEM((SLABS, 8, 768), F32),
             pltpu.VMEM((2, 7, 8, 768), F32),
             pltpu.VMEM((SLABS, 3, 8, 256), F32),
-            dma,
-            dma((2, 7)),
-            dma((2, 7)),
+            dma((3,)),
+            dma((2, 13)),
+            dma((2, 13)),
             dma((2, SLABS)),
             dma((SLABS, 2, 3)),
             dma((SLABS, 2, 3)),
@@ -474,7 +538,7 @@
             dma((SLABS,)),
         ],
         compiler_params=pltpu.CompilerParams(
-            collective_id=0, has_side_effects=True, vmem_limit_bytes=60 << 20
+            collective_id=0, has_side_effects=True, vmem_limit_bytes=52 << 20
         ),
     )(
         features.reshape(cells, channels),
@@ -482,6 +546,14 @@
         conv_weight.reshape(9, 3 * channels, channels),
         cotangent.reshape(cells, channels),
     )
+    decoded, grad_features, grad_weight = pl.pallas_call(
+        finish,
+        out_shape=results,
+        in_specs=[anywhere] * 3,
+        out_specs=[hbm] * 3,
+        scratch_shapes=[dma((3,))],
+        compiler_params=pltpu.CompilerParams(vmem_limit_bytes=4 << 20),
+    )(*held)
     grad_weight = grad_weight.reshape(3, 3, 3, channels // owners, channels).transpose(0, 1, 2, 4, 3)
     return decoded.reshape(features.shape), grad_features.reshape(features.shape), grad_weight
 

time: 82 us -> 63 us (0.77)
  Pallas kernels: 75.7 us -> 60.1 us
  local copies, waits for them, and re-layouts: 5.37 us -> 1.71 us
    pallas_call x1 -> x2, Pallas kernels: 75.7 us -> 60.1 us  [the longest x1 59 us: body(): pl.pallas_call(run, out_shape=results, in_specs=[hbm, vmem, hbm, hbm], ou...]
    unnamed x3 -> x4, local copies, waits for them, and re-layouts: 5.37 us -> 1.71 us
where the time goes in v2:
time: 63 us; the launch traced here: 62.4 us
  Pallas kernels  60.1 us (95%)
  local copies, waits for them, and re-layouts  1.71 us (3%)
  between operations  0.65 us (1%)
    pallas_call x1, Pallas kernels, body(): pl.pallas_call(run, out_shape=results, in_specs=[hbm, vmem, hbm, hbm], ou...  59 us
    unnamed x4, local copies, waits for them, and re-layouts  1.71 us

profile of v2, /device:TPU:1, one launch (start us, length us, event | category | flops | bytes accessed | tf_op | source)
XLA Modules:
  0.0 62.4 jit_solution(14511623029443761192)
XLA Ops:
  0.6 0.0 copy-start
  0.6 1.0 %copy-done = bf16[4,16,16,256]{3,2,1,0:T(8,128)(2,1)S(1)} copy-done((bf16[4,16,16,256]{3,2,1,0:T(8,128)(2,1)S(1)}, bf16[4,16,16,256]{3,2,1,0:T(8,128)(2,1)}, u32[]{:S(2)}) %copy-start) | copy-done | bytes 524312
  1.7 0.0 copy-start.1
  1.7 0.7 %copy-done.1 = f32[256]{0:T(256)S(1)} copy-done((f32[256]{0:T(256)S(1)}, f32[256]{0:T(256)}, u32[]{:S(2)}) %copy-start.1) | copy-done | bytes 1048
  2.4 59.0 %shard_map.67 = (bf16[1024,256]{1,0:T(8,128)(2,1)S(1)}, bf16[1024,256]{1,0:T(8,128)(2,1)S(1)}, f32[27,8,256]{2,1,0:T(8,128)S(1)}) custom-call(bf16[1024,256]{1,0:T(8,128)(2,1)S(1)} %bitcast.9, f32[1,256]{1,0:T(1,128)S(1)} %bitcast.10, bf16[9,768,256]{2,1,0:T(8,128)(2,1)} %bitcast.11, bf16[1024,256]{1,0:T(8,128)(2,1)} %bitcast.12), custom_call_target="tpu_custom_call" | custom-call | tf_op jit(solution)/shard_map/pallas_call | solution.py:496
  61.4 1.1 %shard_map.68 = (bf16[1024,256]{1,0:T(8,128)(2,1)}, bf16[1024,256]{1,0:T(8,128)(2,1)}, f32[27,8,256]{2,1,0:T(8,128)}) custom-call(bf16[1024,256]{1,0:T(8,128)(2,1)S(1)} %get-tuple-element.9.refs_0_, bf16[1024,256]{1,0:T(8,128)(2,1)S(1)} %get-tuple-element.10.refs_1_, f32[27,8,256]{2,1,0:T(8,128)S(1)} %get-tuple-element.11.refs_2_), custom_call_target="tpu_custom_call" | custom-call | tf_op jit(solution)/shard_map/pallas_call | solution.py:549
Async XLA Ops:
  0.6 1.0 %copy-start = (bf16[4,16,16,256]{3,2,1,0:T(8,128)(2,1)S(1)}, bf16[4,16,16,256]{3,2,1,0:T(8,128)(2,1)}, u32[]{:S(2)}) copy-start(bf16[4,16,16,256]{3,2,1,0:T(8,128)(2,1)} %param.4) | copy-start | bytes 1572868
  1.7 0.7 %copy-start.1 = (f32[256]{0:T(256)S(1)}, f32[256]{0:T(256)}, u32[]{:S(2)}) copy-start(f32[256]{0:T(256)} %param.5) | copy-start | bytes 3076

commit v3 on v2

v3 whole, which is shorter than its diff:
```python
import jax
import jax.numpy as jnp
from jax import lax
from jax.experimental import pallas as pl
from jax.experimental.pallas import tpu as pltpu
from jax.sharding import PartitionSpec as P

EPSILON = 1e-06
MESH = pl.DeviceIdType.MESH
F32 = jnp.float32
BF16 = jnp.bfloat16
SLABS = 9
OWNED = 8
ROW = 18 * 16
PADDED = 6 * ROW
TICKS = 34


def dot(a, b):
    return jnp.dot(a, b, preferred_element_type=F32)


def wrap(value, count):
    return lax.rem(value + count, count)


def remote(src, dst, send, recv, device):
    return pltpu.make_async_remote_copy(
        src_ref=src, dst_ref=dst, send_sem=send, recv_sem=recv, device_id=device, device_id_type=MESH
    )


def normalise(cells, gain):
    values = cells.astype(F32)
    inverse = lax.rsqrt(jnp.mean(values * values, axis=-1, keepdims=True) + EPSILON)
    unit = values * inverse
    return values, inverse, unit, unit * gain


def kernel(
    scale,
    feat_hbm,
    gain_hbm,
    weight_hbm,
    cot_hbm,
    decoded,
    grad_feat,
    grad_weight,
    gain,
    feat,
    cot,
    act,
    grd,
    act3,
    grd3,
    cot_t,
    weight,
    select,
    put,
    shift,
    edge,
    halo,
    halo_t,
    mixed,
    back,
    part,
    pair,
    send1,
    recv1,
    mid,
    send2,
    recv2,
    flat,
    recv3,
    every,
    total,
    load_sem,
    halo_send,
    halo_recv,
    pair_sem,
    send1_sem,
    recv1_sem,
    send2_sem,
    recv2_sem,
    flat_sem,
    recv3_sem,
    every_send,
    every_recv,
    total_send,
    total_recv,
):
    t = lax.axis_index("ta")
    ha = lax.axis_index("ha")
    wa = lax.axis_index("wa")
    core = lax.rem(ha, 2)
    x = (ha // 2) * 2 + wa // 4
    y = lax.rem(wa, 4)

    def at(z, xx, cc, yy):
        return (z, (xx // 2) * 2 + cc, lax.rem(xx, 2) * 4 + yy)

    def near(dt, dh, dw):
        return (wrap(t + dt, 8), wrap(ha + dh, 4), wrap(wa + dw, 8))

    around = [(dh, dw) for dh in (-1, 0, 1) for dw in (-1, 0, 1) if (dh, dw) != (0, 0)]
    partners = [near(dt, dh, dw) for dt in (-1, 0, 1) for dh, dw in around]
    partners += [at(t, x, 1 - core, y)]
    partners += [at(t, wrap(x + k, 4), core, y) for k in (1, 2, 3)]
    partners += [at(t, x, core, wrap(y + k, 4)) for k in (1, 2, 3)]
    partners += [near(k, 0, 0) for k in range(1, 8)]
    barrier = pltpu.get_barrier_semaphore()
    for device in partners:
        pl.semaphore_signal(barrier, inc=1, device_id=device, device_id_type=MESH)

    loads = [
        pltpu.make_async_copy(far, here, load_sem.at[n])
        for n, (far, here) in enumerate(((feat_hbm, feat), (cot_hbm, cot), (weight_hbm, weight), (gain_hbm, gain)))
    ]
    for load in loads:
        load.start()

    def ones(condition):
        return jnp.where(condition, 1.0, 0.0).astype(BF16)

    line = lax.broadcasted_iota(jnp.int32, (96, 1024), 0)
    cell = lax.broadcasted_iota(jnp.int32, (96, 1024), 1)
    first_column = jnp.where(line < 64, line * 16, (line & 15) * 256 + jnp.where(line < 80, 240, 0))
    usable = (line < 64) | ((line & 15) < 4)
    select[0] = ones(usable & (cell == first_column + 15))
    select[1] = ones(usable & (cell == first_column))
    loads[3].wait()
    loads[0].wait()

    @pl.loop(0, 16)
    def _(n):
        rows = pl.ds(pl.multiple_of(n * 64, 64), 64)
        normed = normalise(feat[rows, :], gain[...])[3]
        act[2 + n // 4, pl.ds(pl.multiple_of(lax.rem(n, 4) * 64 + 16, 16), 64), :] = (
            normed * jax.nn.sigmoid(normed)
        ).astype(BF16)

    for n in range(2):
        for side in range(2):
            unused = pl.ds(32 * n, 32)
            halo_t[n, side, unused] = jnp.zeros((32, 256), BF16)

    pl.semaphore_wait(barrier, len(partners))

    def rows_of(ref, frame, frames, row, rows):
        return ref.at[pl.ds(frame, frames), pl.ds(row * 16, rows * 16), :]

    frame_moves = []
    row_moves = []
    column_moves = []
    for n, (ref, dt, own, ends) in enumerate(((act, 1, 2, ((5, 1), (4, 0))), (grd, -1, 0, ((0, 4), (1, 5))))):
        at_sem = iter(range(18))

        def move(source, target, device):
            m = next(at_sem)
            return remote(source, target, halo_send.at[n, m], halo_recv.at[n, m], device)

        frame_moves.append(
            [
                move(
                    rows_of(ref, a, 1, 1, 16) if n == 0 else cot.at[pl.ds(a * 256, 256)].reshape(1, 256, 256),
                    rows_of(ref, b, 1, 1, 16),
                    near(dt, 0, 0),
                )
                for a, b in ends
            ]
        )
        (a0, b0), (a1, b1) = ends
        a, b = min(a0, a1), min(b0, b1)
        row_moves.append(
            [
                [
                    move(rows_of(ref, source, count, row, 1), rows_of(ref, target, count, row - 16 * dh, 1), near(d, dh, 0))
                    for dh, row in ((1, 16), (-1, 1))
                ]
                for d, source, target, count in ((0, own, own, 4), (dt, a, b, 2))
            ]
        )
        column_moves.append(
            [
                [
                    move(edge.at[n, side, pl.ds(begin, count)], borders.at[n, side, pl.ds(begin, count)], near(d, dh, dw))
                    for side, dw in ((0, 1), (1, -1))
                    for begin, count, dh in (main, (64, 16, 1), (80, 16, -1))
                ]
                for d, borders, main in ((0, halo, (0, 64, 0)), (dt, halo_t, ((a - own) * 16, 32, 0)))
            ]
        )

    def start(copies):
        for copy in copies:
            copy.start()

    def take(copies):
        for copy in copies:
            copy.wait_recv()

    def edges(n, own):
        for side in range(2):
            acc = None
            for f in range(4):
                term = dot(select[side, :, f * 256 : f * 256 + 256], own[f][...])
                acc = term if acc is None else acc + term
            edge[n, side] = acc.astype(BF16)

    start(frame_moves[0][:1])
    loads[1].wait()
    start(frame_moves[1][:1])
    start(row_moves[0][0] + row_moves[0][1])
    edges(0, [act.at[n + 2, 16:272] for n in range(4)])
    start(column_moves[0][0] + column_moves[0][1])

    for n in range(4):
        grd[n, 16:272, :] = cot[n * 256 : n * 256 + 256, :]
    start(frame_moves[0][1:])
    start(row_moves[1][0] + row_moves[1][1])
    edges(1, [cot.at[n * 256 : n * 256 + 256] for n in range(4)])
    start(column_moves[1][0] + column_moves[1][1])
    start(frame_moves[1][1:])
    for n in range(4):
        line = lax.broadcasted_iota(jnp.int32, (ROW, 96), 1)
        cell = lax.broadcasted_iota(jnp.int32, (ROW, 96), 0)
        row = jnp.where(line < 64, (line & 15) + 1, jnp.where(line < 80, 0, 17))
        frame = jnp.where(line < 64, line // 16, line & 15)
        put[0, n] = ones((frame == n) & (cell == row * 16))
        put[1, n] = ones((frame == n) & (cell == row * 16 + 15))
    cell = lax.broadcasted_iota(jnp.int32, (ROW, ROW), 0)
    other = lax.broadcasted_iota(jnp.int32, (ROW, ROW), 1)
    column = cell & 15
    shift[0] = ones((cell == other + 1) & (column != 0))
    shift[1] = ones((cell == other - 1) & (column != 15))

    for n in range(4):
        cot_t[n] = cot[n * 256 : (n + 1) * 256, :].T
    mixed[...] = jnp.zeros_like(mixed)
    back[...] = jnp.zeros_like(back)

    def clear(n, ref, borders, begin, frames):
        @pl.when(ha == 0)
        def _():
            for frame in range(frames):
                ref[begin + frame, 0:16, :] = jnp.zeros((16, 256), BF16)
            for side in range(2):
                borders[n, side, 64:80] = jnp.zeros((16, 256), BF16)

        @pl.when(ha == 3)
        def _():
            for frame in range(frames):
                ref[begin + frame, 272:288, :] = jnp.zeros((16, 256), BF16)
            for side in range(2):
                borders[n, side, 80:96] = jnp.zeros((16, 256), BF16)

        @pl.when(wa == 0)
        def _():
            borders[n, 0] = jnp.zeros((96, 256), BF16)

        @pl.when(wa == 7)
        def _():
            borders[n, 1] = jnp.zeros((96, 256), BF16)

    def clear_frame(ref, frame, at_end):
        @pl.when(at_end)
        def _():
            ref[frame] = jnp.zeros((ROW, 256), BF16)

    def take_near(n, ref, own):
        take(row_moves[n][0] + column_moves[n][0])
        clear(n, ref, halo, own, 4)

    def take_far(n, ref, far, at_end):
        take(row_moves[n][1] + column_moves[n][1])
        clear(n, ref, halo_t, far, 2)

        @pl.when(at_end)
        def _():
            for side in range(2):
                halo_t[n, side] = jnp.zeros((96, 256), BF16)

    def widen(n, ref, wide, frame, own, borders):
        rows = pl.ds(pl.multiple_of(frame * ROW, 16), ROW)
        wide[rows, 256:512] = ref[frame]
        for side, lanes in ((0, 0), (1, 512)):
            moved = dot(shift[side], ref[frame]) + dot(put[side, own], borders[n, side])
            wide[rows, lanes : lanes + 256] = moved.astype(BF16)

    take_near(0, act, 2)

    @pl.loop(0, 4)
    def _(frame):
        widen(0, act, act3, frame + 2, frame, halo)

    def to_pair(s):
        return remote(
            part.at[s, :, 1 - core], pair.at[s], pair_sem.at[0, s], pair_sem.at[1, s], at(t, x, 1 - core, y)
        )

    def along(half, k):
        return at(t, wrap(x + k, 4), core, y) if half == 0 else at(t, x, core, wrap(y + k, 4))

    def copy1(s, half, k):
        slot = wrap((x if half == 0 else y) + k, 4)
        return remote(
            send1.at[s, half, slot],
            recv1.at[s, half, k - 1],
            send1_sem.at[s, half, k - 1],
            recv1_sem.at[s, half, k - 1],
            along(half, k),
        )

    def copy2(s, half, k):
        slot = wrap((y if half == 0 else x) + k, 4)
        return remote(
            send2.at[s, half, slot],
            recv2.at[s, half, k - 1],
            send2_sem.at[s, half, k - 1],
            recv2_sem.at[s, half, k - 1],
            along(1 - half, k),
        )

    def stage_gradient(s):
        i, j = 2 - s // 3, lax.rem(s, 3)
        acc = None
        for n in range(4):
            frame, pairs = n + i, n
            if n == 0:
                frame, pairs = jnp.where(i == 0, 4, i), jnp.where(i == 0, 4, 0)
            rows = pl.ds(pl.multiple_of(frame * ROW + j * 16, 16), 256)
            term = dot(cot_t[pairs], act3[rows, :])
            acc = term if acc is None else acc + term
        part[s] = acc.reshape(2, 2, 64, 768)
        to_pair(s).start()

    def stage_first(s):
        to_pair(s).wait_recv()
        for n in range(2):
            pair[s, n] = pair[s, n] + part[s, n, core]
        for d in range(4):
            n, r = d // 2, (d % 2) * 32
            send1[s, 0, d] = pair[s, n, r : r + 32, 0:384].astype(BF16)
            rows = [pair[s, e // 2, (e % 2) * 32 + d * 8 : (e % 2) * 32 + d * 8 + 8, 384:768] for e in range(4)]
            send1[s, 1, d] = jnp.concatenate(rows, axis=0).astype(BF16)
        for k in (2, 1, 3):
            for half in range(2):
                copy1(s, half, k).start()

    def stage_second(s):
        for half in range(2):
            for k in (1, 2, 3):
                copy1(s, half, k).wait_recv()
        own = pair[s, x // 2, pl.ds(pl.multiple_of(lax.rem(x, 2) * 32, 32), 32), 0:384]
        for k in range(3):
            own = own + recv1[s, 0, k].astype(F32)
        mid[s, 0] = own.reshape(4, 8, 384)
        send2[s, 0] = own.reshape(4, 8, 384).astype(BF16)
        rows = [
            pair[s, e // 2, pl.ds(pl.multiple_of((e % 2) * 32 + y * 8, 8), 8), 384:768] for e in range(4)
        ]
        own = jnp.concatenate(rows, axis=0)
        for k in range(3):
            own = own + recv1[s, 1, k].astype(F32)
        mid[s, 1] = own.reshape(4, 8, 384)
        send2[s, 1] = own.reshape(4, 8, 384).astype(BF16)
        for k in (2, 1, 3):
            for half in range(2):
                copy2(s, half, k).start()

    def owner_of(s, tile):
        return lax.rem(6 * s + tile, 8)

    def owned(s):
        return lax.rem(t + 2 * s, 8)

    def to_owner(s, tile):
        owner = owner_of(s, tile)
        k = wrap(t - owner - 1, 8)
        return remote(flat.at[s, tile], recv3.at[s, k], flat_sem.at[s, tile], recv3_sem.at[s, k], (owner, ha, wa))

    def from_owner(s, tile, k):
        place = total.at[s, tile]
        return remote(place, place, total_send.at[s, k - 1], total_recv.at[s, tile], near(k, 0, 0))

    def to_every(s, k):
        place = every.at[s - OWNED, t]
        return remote(place, place, every_send.at[s - OWNED, k - 1], every_recv.at[s - OWNED, t], near(k, 0, 0))

    def second_sums(s):
        for half in range(2):
            for k in (1, 2, 3):
                copy2(s, half, k).wait_recv()
        sums = []
        for half, slot in ((0, y), (1, x)):
            own = mid[s, half, slot]
            for k in range(3):
                own = own + recv2[s, half, k].astype(F32)
            sums.append(own)
        return sums

    def stage_third(s):
        sums = second_sums(s)
        for half in range(2):
            for k in range(3):
                flat[s, half * 3 + k] = sums[half][:, k * 128 : k * 128 + 128]
        for tile in range(6):

            @pl.when(t != owner_of(s, tile))
            def _():
                to_owner(s, tile).start()

    def stage_every(n):
        s = n + OWNED
        sums = second_sums(s)
        for half in range(2):
            every[n, t, :, half * 384 : half * 384 + 384] = sums[half].astype(BF16)
        for k in (4, 3, 5, 2, 6, 1, 7):
            to_every(s, k).start()

    def stage_owner(s):
        tile = owned(s)

        @pl.when(tile < 6)
        def _():
            own = flat[s, tile]
            for k in range(7):
                remote(
                    flat.at[s, 0], recv3.at[s, k], flat_sem.at[s, 0], recv3_sem.at[s, k], near(1, 0, 0)
                ).wait_recv()
                own = own + recv3[s, k]
            total[s, tile] = own * scale
            for k in (4, 3, 5, 2, 6, 1, 7):
                from_owner(s, tile, k).start()

    def stage_weight(_):
        loads[2].wait()

    def stage_mixed(s):
        i, j = 2 - s // 3, lax.rem(s, 3)
        for n in range(4):
            rows = pl.ds(pl.multiple_of((n + i) * ROW + j * 16, 16), 256)
            mixed[n * 256 : n * 256 + 256, :] += dot(act3[rows, :], weight[i * 3 + j])

    def stage_back(s):
        i, j = 2 - s // 3, lax.rem(s, 3)
        for n in range(4):
            rows = pl.ds(pl.multiple_of((n + 2 - i) * ROW + (2 - j) * 16, 16), 256)
            acc = None
            for k in range(3):
                term = lax.dot_general(
                    grd3[rows, (2 - k) * 256 : (3 - k) * 256],
                    weight[i * 3 + j, k * 256 : k * 256 + 256, :],
                    (((1,), (1,)), ((), ())),
                    preferred_element_type=F32,
                )
                acc = term if acc is None else acc + term
            back[n * 256 : n * 256 + 256, :] += acc

    def stage_act(_):
        take_far(0, act, 0, t == 0)
        take(frame_moves[0][:1])
        clear_frame(act, 1, t == 0)
        widen(0, act, act3, 1, 3, halo_t)
        take(frame_moves[1][:1])
        cot_t[4] = grd[4, 16:272, :].T

        @pl.when(t == 7)
        def _():
            cot_t[4] = jnp.zeros((256, 256), BF16)


    def stage_act_last(_):
        take(frame_moves[0][1:])
        clear_frame(act, 0, t == 0)
        widen(0, act, act3, 0, 2, halo_t)

    def stage_cot_near(_):
        take_near(1, grd, 0)

    def stage_cot(frame):
        widen(1, grd, grd3, frame, frame, halo)

    def stage_cot_late(_):
        take_far(1, grd, 4, t == 7)
        take(frame_moves[1][1:])
        for frame in (4, 5):
            clear_frame(grd, frame, t == 7)
        for frame in range(2):
            widen(1, grd, grd3, frame + 4, frame, halo_t)

    def stage_decoded(n):
        for m in range(4):
            rows = pl.ds(pl.multiple_of(n * 256 + m * 64, 64), 64)
            decoded[rows, :] = (feat[rows, :].astype(F32) + mixed[rows, :]).astype(BF16)

    def stage_grad(n):
        @pl.loop(0, 4)
        def _(m):
            rows = pl.ds(pl.multiple_of(n * 256 + m * 64, 64), 64)
            _, inverse, unit, normed = normalise(feat[rows, :], gain[...])
            logistic = jax.nn.sigmoid(normed)
            grad_unit = back[rows, :] * logistic * (1.0 + normed * (1.0 - logistic)) * gain[...]
            grad = inverse * (grad_unit - unit * jnp.mean(grad_unit * unit, axis=-1, keepdims=True))
            grad_feat[rows, :] = (cot[rows, :].astype(F32) + grad).astype(BF16)

    plan = (
        (stage_act, 3, 1, 1, 1),
        (stage_gradient, 0, 1, 1, SLABS),
        (stage_first, 2, 1, 1, SLABS),
        (stage_second, 8, 1, 1, SLABS),
        (stage_third, 13, 1, 1, OWNED),
        (stage_every, 21, 1, 1, SLABS - OWNED),
        (stage_owner, 20, 1, 1, OWNED),
        (stage_weight, 11, 1, 1, 1),
        (stage_cot_near, 9, 1, 1, 1),
        (stage_cot, 12, 1, 1, 4),
        (stage_act_last, 16, 1, 1, 1),
        (stage_cot_late, 17, 1, 1, 1),
        (stage_mixed, 11, 1, 1, SLABS),
        (stage_back, 20, 1, 1, SLABS),
        (stage_decoded, 21, 2, 1, 4),
        (stage_grad, 30, 1, 1, 4),
    )

    @pl.loop(0, TICKS)
    def _(tick):
        for stage, begin, over, under, count in plan:
            past = tick - begin
            n = (jnp.maximum(past, 0) * under + over - 1) // over

            @pl.when((past >= 0) & (n < count) & ((n * over) // under == past))
            def _():
                stage(n)

    @pl.loop(0, SLABS)
    def _(s):
        to_pair(s).wait_send()
        for half in range(2):
            for k in (1, 2, 3):
                copy1(s, half, k).wait_send()
                copy2(s, half, k).wait_send()

    def taps(s):
        return (2 - s // 3) * 9 + lax.rem(s, 3) * 3

    @pl.loop(0, OWNED)
    def _(s):
        for tile in range(6):

            @pl.when(t != owner_of(s, tile))
            def _():
                to_owner(s, tile).wait_send()
                from_owner(s, tile, 1).wait_recv()

        @pl.when(owned(s) < 6)
        def _():
            for k in range(1, 8):
                from_owner(s, 0, k).wait_send()

        for k in range(3):
            for n in range(2):
                grad_weight[taps(s) + k, :, n * 128 : n * 128 + 128] = total[s, k * 2 + n]

    @pl.loop(OWNED, SLABS)
    def _(s):
        n = s - OWNED
        for k in range(1, 8):
            place = every.at[n, wrap(t + k, 8)]
            remote(place, place, every_send.at[n, k - 1], every_recv.at[n, wrap(t + k, 8)], near(k, 0, 0)).wait_recv()
        own = every[n, 0].astype(F32)
        for z in range(1, 8):
            own = own + every[n, z].astype(F32)
        own = own * scale
        for k in range(3):
            grad_weight[taps(s) + k] = own[:, k * 256 : k * 256 + 256]
        for k in range(1, 8):
            to_every(s, k).wait_send()

    for n in range(2):
        for copy in frame_moves[n] + sum(row_moves[n] + column_moves[n], []):
            copy.wait_send()


def finish(*refs):
    copies = [pltpu.make_async_copy(refs[n], refs[n + 3], refs[6].at[n]) for n in range(3)]
    for copy in copies:
        copy.start()
    for copy in copies:
        copy.wait()


def body(features, norm_gain, conv_weight, cotangent):
    frames, height, width, channels = features.shape
    cells = frames * height * width
    owners = lax.axis_size("ha") * lax.axis_size("wa")
    voxels = cells * owners * lax.axis_size("ta")
    vmem = pl.BlockSpec(memory_space=pltpu.VMEM)
    hbm = pl.BlockSpec(memory_space=pltpu.HBM)
    anywhere = pl.BlockSpec(memory_space=pl.ANY)
    dma = pltpu.SemaphoreType.DMA

    def run(*refs):
        kernel(float(voxels) ** (-0.5), *refs)

    results = (
        jax.ShapeDtypeStruct((cells, channels), BF16),
        jax.ShapeDtypeStruct((cells, channels), BF16),
        jax.ShapeDtypeStruct((27, channels // owners, channels), F32),
    )
    held = pl.pallas_call(
        run,
        out_shape=results,
        in_specs=[hbm] * 4,
        out_specs=(vmem, vmem, vmem),
        scratch_shapes=[
            pltpu.VMEM((1, 256), F32),
            pltpu.VMEM((1024, 256), BF16),
            pltpu.VMEM((1024, 256), BF16),
            pltpu.VMEM((6, ROW, 256), BF16),
            pltpu.VMEM((6, ROW, 256), BF16),
            pltpu.VMEM((PADDED, 768), BF16),
            pltpu.VMEM((PADDED, 768), BF16),
            pltpu.VMEM((5, 256, 256), BF16),
            pltpu.VMEM((SLABS, 768, 256), BF16),
            pltpu.VMEM((2, 96, 1024), BF16),
            pltpu.VMEM((2, 4, ROW, 96), BF16),
            pltpu.VMEM((2, ROW, ROW), BF16),
            pltpu.VMEM((2, 2, 96, 256), BF16),
            pltpu.VMEM((2, 2, 96, 256), BF16),
            pltpu.VMEM((2, 2, 96, 256), BF16),
            pltpu.VMEM((1024, 256), F32),
            pltpu.VMEM((1024, 256), F32),
            pltpu.VMEM((SLABS, 2, 2, 64, 768), F32),
            pltpu.VMEM((SLABS, 2, 64, 768), F32),
            pltpu.VMEM((SLABS, 2, 4, 32, 384), BF16),
            pltpu.VMEM((SLABS, 2, 3, 32, 384), BF16),
            pltpu.VMEM((SLABS, 2, 4, 8, 384), F32),
            pltpu.VMEM((SLABS, 2, 4, 8, 384), BF16),
            pltpu.VMEM((SLABS, 2, 3, 8, 384), BF16),
            pltpu.VMEM((OWNED, 6, 8, 128), F32),
            pltpu.VMEM((OWNED, 7, 8, 128), F32),
            pltpu.VMEM((SLABS - OWNED, 8, 8, 768), BF16),
            pltpu.VMEM((SLABS, 6, 8, 128), F32),
            dma((4,)),
            dma((2, 18)),
            dma((2, 18)),
            dma((2, SLABS)),
            dma((SLABS, 2, 3)),
            dma((SLABS, 2, 3)),
            dma((SLABS, 2, 3)),
            dma((SLABS, 2, 3)),
            dma((OWNED, 6)),
            dma((OWNED, 7)),
            dma((SLABS - OWNED, 7)),
            dma((SLABS - OWNED, 8)),
            dma((OWNED, 7)),
            dma((OWNED, 6)),
        ],
        compiler_params=pltpu.CompilerParams(
            collective_id=0, has_side_effects=True, vmem_limit_bytes=52 << 20
        ),
    )(
        *(
            pltpu.with_memory_space_constraint(array, pltpu.HBM)
            for array in (
                features.reshape(cells, channels),
                norm_gain.reshape(1, channels),
                conv_weight.reshape(9, 3 * channels, channels),
                cotangent.reshape(cells, channels),
            )
        ),
    )
    decoded, grad_features, grad_weight = pl.pallas_call(
        finish,
        out_shape=results,
        in_specs=[anywhere] * 3,
        out_specs=[hbm] * 3,
        scratch_shapes=[dma((3,))],
        compiler_params=pltpu.CompilerParams(vmem_limit_bytes=4 << 20),
    )(*held)
    grad_weight = grad_weight.reshape(3, 3, 3, channels // owners, channels).transpose(0, 1, 2, 4, 3)
    return decoded.reshape(features.shape), grad_features.reshape(features.shape), grad_weight


def solution(mesh):
    placed = (P("ta", "ha", "wa", None), P(), P(), P("ta", "ha", "wa", None))
    return jax.shard_map(
        body,
        mesh=mesh,
        in_specs=placed,
        out_specs=(
            P("ta", "ha", "wa", None),
            P("ta", "ha", "wa", None),
            P(None, None, None, None, ("ha", "wa")),
        ),
        check_vma=False,
    )
```

time: 63 us -> 59.1 us (0.938)
  local copies, waits for them, and re-layouts: 1.71 us -> 0 us
  Pallas kernels: 60.1 us -> 58.4 us
    unnamed x4 -> x0, local copies, waits for them, and re-layouts: 1.71 us -> none
    pallas_call x1, Pallas kernels: 59 us -> 57.3 us  [body(): pl.pallas_call(run, out_shape=results, in_specs=[hbm] * 4, out_specs=(vme...]
where the time goes in v3:
time: 59.1 us; the launch traced here: 59 us
  Pallas kernels  58.4 us (99%)
  between operations  0.64 us (1%)
    pallas_call x1, Pallas kernels, body(): pl.pallas_call(run, out_shape=results, in_specs=[hbm] * 4, out_specs=(vme...  57.3 us

profile of v3, /device:TPU:1, one launch (start us, length us, event | category | flops | bytes accessed | tf_op | source)
XLA Modules:
  0.0 59.0 jit_solution(1747739282956873642)
XLA Ops:
  0.6 57.3 %shard_map.67 = (bf16[1024,256]{1,0:T(8,128)(2,1)S(1)}, bf16[1024,256]{1,0:T(8,128)(2,1)S(1)}, f32[27,8,256]{2,1,0:T(8,128)S(1)}) custom-call(bf16[1024,256]{1,0:T(8,128)(2,1)} %bitcast.10, f32[1,256]{1,0:T(1,128)} %bitcast.12, bf16[9,768,256]{2,1,0:T(8,128)(2,1)} %bitcast.9, bf16[1024,256]{1,0:T(8,128)(2,1)} %bitcast.11), custom_call_target="tpu_custom_call" | custom-call | tf_op jit(solution)/shard_map/pallas_call | solution.py:611
  58.0 1.1 %shard_map.68 = (bf16[1024,256]{1,0:T(8,128)(2,1)}, bf16[1024,256]{1,0:T(8,128)(2,1)}, f32[27,8,256]{2,1,0:T(8,128)}) custom-call(bf16[1024,256]{1,0:T(8,128)(2,1)S(1)} %get-tuple-element.9.refs_0_, bf16[1024,256]{1,0:T(8,128)(2,1)S(1)} %get-tuple-element.10.refs_1_, f32[27,8,256]{2,1,0:T(8,128)S(1)} %get-tuple-element.11.refs_2_), custom_call_target="tpu_custom_call" | custom-call | tf_op jit(solution)/shard_map/pallas_call | solution.py:674
